TPU v7x, 32 devices: a whole 2x2x4 slice. The times are simulated.
32 devices in a mesh: leaf: 8 (over z, y), fsdp: 4 (over x, core).
Axes of the slice: x: 2, y: 2, z: 4, core: 2. Of those that a mesh axis runs over, the one named last changes fastest.
Arguments:
- hidden: bfloat16 [4, 2048, 768], P('fsdp', 'leaf'), may hold values from -6 to 6
- noise_mask: int32 [4, 2048], P('fsdp', 'leaf'), may hold values 0 or 1
- seg_blocks: int32 [4, 128], P('fsdp'), may hold values from 0 to 12, as said below
- parents: int32 [4, 13], P('fsdp'), may hold values from 0 to 4, as said below
- ln1_gain: bfloat16 [768], P(('leaf', 'fsdp')), may hold values from 0.099609375 to 1.8984375
- w_qkv: bfloat16 [768, 2304], P(('leaf', 'fsdp')), may hold values from -0.21875 to 0.21875
- w_out: bfloat16 [768, 768], P(('leaf', 'fsdp')), may hold values from -3.5 to 3.5
- ln2_gain: bfloat16 [768], P(('leaf', 'fsdp')), may hold values from 0.099609375 to 1.8984375
- w_up: bfloat16 [768, 3072], P(('leaf', 'fsdp')), may hold values from -0.21875 to 0.21875
- up_bias: bfloat16 [3072], P(('leaf', 'fsdp')), may hold values from -3 to 3
- w_down: bfloat16 [3072, 768], P(('leaf', 'fsdp')), may hold values from -0.109375 to 0.109375
- down_bias: bfloat16 [768], P(('leaf', 'fsdp')), may hold values from -2 to 2
- mask_embed: bfloat16 [768], P(('leaf', 'fsdp')), may hold values from -5 to 5
- cotangent: bfloat16 [4, 2, 2048, 768], P('fsdp', None, 'leaf'), may hold values from -6 to 6
Outputs:
- output: bfloat16 [4, 2, 2048, 768], P('fsdp', None, 'leaf')
- grad_hidden: bfloat16 [4, 2048, 768], P('fsdp', 'leaf')
- grad_ln1_gain: float32 [768], P(('leaf', 'fsdp'))
- grad_w_qkv: float32 [768, 2304], P(('leaf', 'fsdp'))
- grad_w_out: float32 [768, 768], P(('leaf', 'fsdp'))
- grad_ln2_gain: float32 [768], P(('leaf', 'fsdp'))
- grad_w_up: float32 [768, 3072], P(('leaf', 'fsdp'))
- grad_up_bias: float32 [3072], P(('leaf', 'fsdp'))
- grad_w_down: float32 [3072, 768], P(('leaf', 'fsdp'))
- grad_down_bias: float32 [768], P(('leaf', 'fsdp'))
- grad_mask_embed: float32 [768], P(('leaf', 'fsdp'))
Inputs may be any that keep to these rules, and one draw needn't show every extreme that they name: `seg_blocks`: segment numbers never fall along a tree; segment 0 holds the first 64 blocks (rounded down); every other segment has one block or more; the last segment ends the tree. `parents`: segment 0 is the trunk with parent 0; segments 1 to 4 have parent 0; each of them is the parent of exactly 2 of the segments above 4.
All inputs are finite; a program needn't handle non-finite values. No bound on the sum of `noise_mask` on one device may be relied on, other than what follows from the above.
Results may differ from a plain program's by a relative error of at most 0.015.
Values may be sent and summed in bfloat16 or wider, within the bound.
No kernel may reach another device: no remote copies, remote signals or barrier semaphores. Data moves between devices by JAX's collectives and lax.ppermute only.
A program may use at most 256 MiB of HBM per device.

v0:
```python
import math
import jax
import jax.numpy as jnp
from jax import lax
from jax.sharding import PartitionSpec as P

HEAD_DIM = 64
BLOCK = 16
NEG_FILL = -1000000000.0
EPSILON = 1e-05


def look_up(table, indices):
    slots = jnp.arange(table.shape[0], dtype=jnp.int32)
    hits = indices[..., None] == slots
    return jnp.sum(jnp.where(hits, table, 0), axis=-1)


def tree_layout(seg_row, parent_row):
    slots = jnp.arange(parent_row.shape[0], dtype=jnp.int32)
    seg_lengths = jnp.sum((seg_row[:, None] == slots).astype(jnp.int32), axis=0)
    seg_starts = jnp.cumsum(seg_lengths) - seg_lengths
    grand_parent = look_up(parent_row, parent_row)
    offsets = jnp.where(slots > 0, look_up(seg_lengths, parent_row), 0) + jnp.where(
        parent_row > 0, look_up(seg_lengths, grand_parent), 0
    )
    block_ids = jnp.arange(seg_row.shape[0], dtype=jnp.int32)
    path_block = look_up(offsets, seg_row) + block_ids - look_up(seg_starts, seg_row)
    return (path_block, look_up(parent_row, seg_row), look_up(grand_parent, seg_row))


def layer_norm(values, gain):
    centred = values - jnp.mean(values, axis=-1, keepdims=True)
    spread = jnp.mean(centred * centred, axis=-1, keepdims=True)
    return centred * lax.rsqrt(spread + EPSILON) * gain


def gelu_tanh(values):
    return jax.nn.gelu(values, approximate=True)


def rotate(values, cosine, sine):
    half = values.shape[-1] // 2
    first = values[..., :half]
    second = values[..., half:]
    return jnp.concatenate(
        [first * cosine - second * sine, second * cosine + first * sine], axis=-1
    )


def to_heads(values, heads):
    return values.reshape(values.shape[0], heads, HEAD_DIM).transpose(1, 0, 2)


def from_heads(values):
    return values.transpose(1, 0, 2).reshape(values.shape[1], values.shape[0] * values.shape[2])


def shards(
    hidden,
    noise_mask,
    seg_blocks,
    parents,
    ln1_gain,
    w_qkv,
    w_out,
    ln2_gain,
    w_up,
    up_bias,
    w_down,
    down_bias,
    mask_embed,
    cotangent,
):
    gathered = (
        lax.all_gather(ln1_gain, ("leaf", "fsdp"), axis=0, tiled=True),
        lax.all_gather(w_qkv, ("leaf", "fsdp"), axis=0, tiled=True),
        lax.all_gather(w_out, ("leaf", "fsdp"), axis=0, tiled=True),
        lax.all_gather(ln2_gain, ("leaf", "fsdp"), axis=0, tiled=True),
        lax.all_gather(w_up, ("leaf", "fsdp"), axis=0, tiled=True),
        lax.all_gather(up_bias, ("leaf", "fsdp"), axis=0, tiled=True),
        lax.all_gather(w_down, ("leaf", "fsdp"), axis=0, tiled=True),
        lax.all_gather(down_bias, ("leaf", "fsdp"), axis=0, tiled=True),
        lax.all_gather(mask_embed, ("leaf", "fsdp"), axis=0, tiled=True),
    )
    gain_one, qkv_w, out_w, gain_two, up_w, up_b, down_w, down_b, embed = gathered
    rows_dev = hidden.shape[1]
    width = hidden.shape[2]
    heads = width // HEAD_DIM
    blocks_dev = rows_dev // BLOCK
    leaf_rank = lax.axis_index("leaf")
    seg_row = seg_blocks[0]
    path_block, first_up, second_up = tree_layout(seg_row, parents[0])
    first_block = leaf_rank * blocks_dev
    own_seg = lax.dynamic_slice_in_dim(seg_row, first_block, blocks_dev)
    own_path = lax.dynamic_slice_in_dim(path_block, first_block, blocks_dev)
    own_first = lax.dynamic_slice_in_dim(first_up, first_block, blocks_dev)
    own_second = lax.dynamic_slice_in_dim(second_up, first_block, blocks_dev)
    related = (
        (seg_row[None, :] == own_seg[:, None])
        | (seg_row[None, :] == own_first[:, None])
        | (seg_row[None, :] == own_second[:, None])
    )
    clean_ok = related & (path_block[None, :] <= own_path[:, None])
    noisy_ok = related & (path_block[None, :] < own_path[:, None])
    clean_tok = jnp.repeat(jnp.repeat(clean_ok, BLOCK, axis=0), BLOCK, axis=1)
    noisy_tok = jnp.repeat(jnp.repeat(noisy_ok, BLOCK, axis=0), BLOCK, axis=1)
    row_block = jnp.arange(rows_dev, dtype=jnp.int32) // BLOCK
    same_block = row_block[:, None] == row_block[None, :]
    mask_all = jnp.concatenate(
        [
            jnp.concatenate([clean_tok, jnp.zeros_like(same_block)], axis=1),
            jnp.concatenate([noisy_tok, same_block], axis=1),
        ],
        axis=0,
    )
    offsets_in = jnp.arange(BLOCK, dtype=jnp.int32)
    positions = (own_path[:, None] * BLOCK + offsets_in).reshape(rows_dev).astype(jnp.float32)
    positions = jnp.concatenate([positions, positions])
    freqs = jnp.exp(
        jnp.arange(HEAD_DIM // 2, dtype=jnp.float32) * (-math.log(10000.0) / (HEAD_DIM // 2))
    )
    angles = positions[:, None, None] * freqs
    cosine = jnp.cos(angles)
    sine = jnp.sin(angles)
    clean = hidden[0].astype(jnp.float32)
    masked = (noise_mask[0] == 1)[:, None]
    noisy = jnp.where(masked, embed.astype(jnp.float32)[None, :], clean)
    stream = jnp.concatenate([clean, noisy], axis=0)
    gain_one_f = gain_one.astype(jnp.float32)
    gain_two_f = gain_two.astype(jnp.float32)
    normed_one = layer_norm(stream, gain_one_f).astype(jnp.bfloat16)
    projected = jnp.dot(normed_one, qkv_w, preferred_element_type=jnp.float32)
    query = rotate(
        projected[:, :width].reshape(2 * rows_dev, heads, HEAD_DIM), cosine, sine
    ).reshape(2 * rows_dev, width)
    keyed = rotate(
        projected[:, width : 2 * width].reshape(2 * rows_dev, heads, HEAD_DIM), cosine, sine
    ).reshape(2 * rows_dev, width)
    query_low = query.astype(jnp.bfloat16)
    key_low = keyed.astype(jnp.bfloat16)
    value_low = projected[:, 2 * width :].astype(jnp.bfloat16)
    tree_keys, tree_values = (
        lax.all_gather(key_low[:rows_dev], "leaf", axis=0, tiled=True),
        lax.all_gather(value_low[:rows_dev], "leaf", axis=0, tiled=True),
    )
    tree_tok = tree_keys.shape[0]
    keys_all = jnp.concatenate([tree_keys, key_low[rows_dev:]], axis=0)
    values_all = jnp.concatenate([tree_values, value_low[rows_dev:]], axis=0)
    q_heads = to_heads(query_low, heads)

    def head_forward(operands):
        q_head, k_head, v_head = operands
        raw = jnp.einsum("qd,kd->qk", q_head, k_head, preferred_element_type=jnp.float32) * 0.125
        scores = jnp.where(mask_all, raw, NEG_FILL)
        top_score = jnp.max(scores, axis=-1, keepdims=True)
        expd = jnp.exp(scores - top_score)
        total = jnp.sum(expd, axis=-1, keepdims=True)
        probs = (expd / total).astype(jnp.bfloat16)
        return (
            jnp.dot(probs, v_head, preferred_element_type=jnp.float32),
            top_score + jnp.log(total),
        )

    attended, log_norm = lax.map(
        head_forward, (q_heads, to_heads(keys_all, heads), to_heads(values_all, heads))
    )
    mixed_low = from_heads(attended).astype(jnp.bfloat16)
    after = stream + jnp.dot(mixed_low, out_w, preferred_element_type=jnp.float32)
    normed_two = layer_norm(after, gain_two_f).astype(jnp.bfloat16)
    pre_act = jnp.dot(normed_two, up_w, preferred_element_type=jnp.float32) + up_b.astype(
        jnp.float32
    )
    activated = gelu_tanh(pre_act).astype(jnp.bfloat16)
    result = (
        after
        + jnp.dot(activated, down_w, preferred_element_type=jnp.float32)
        + down_b.astype(jnp.float32)
    )
    output = result.astype(jnp.bfloat16).reshape(1, 2, rows_dev, width)
    regathered = (
        lax.all_gather(ln1_gain, ("leaf", "fsdp"), axis=0, tiled=True),
        lax.all_gather(w_qkv, ("leaf", "fsdp"), axis=0, tiled=True),
        lax.all_gather(w_out, ("leaf", "fsdp"), axis=0, tiled=True),
        lax.all_gather(ln2_gain, ("leaf", "fsdp"), axis=0, tiled=True),
        lax.all_gather(w_up, ("leaf", "fsdp"), axis=0, tiled=True),
        lax.all_gather(up_bias, ("leaf", "fsdp"), axis=0, tiled=True),
        lax.all_gather(w_down, ("leaf", "fsdp"), axis=0, tiled=True),
        lax.all_gather(down_bias, ("leaf", "fsdp"), axis=0, tiled=True),
        lax.all_gather(mask_embed, ("leaf", "fsdp"), axis=0, tiled=True),
    )
    qkv_back, out_back, up_back, down_back = (
        regathered[1],
        regathered[2],
        regathered[4],
        regathered[6],
    )
    grad_out = cotangent[0].astype(jnp.float32).reshape(2 * rows_dev, width)
    grad_two = grad_out.astype(jnp.bfloat16)
    grad_down_b = jnp.sum(grad_two.astype(jnp.float32), axis=0)
    grad_down_w = jnp.einsum("rf,rd->fd", activated, grad_two, preferred_element_type=jnp.float32)
    grad_act = jnp.einsum("rd,fd->rf", grad_two, down_back, preferred_element_type=jnp.float32)
    gelu_out, gelu_back = jax.vjp(gelu_tanh, pre_act)
    grad_pre = gelu_back(grad_act)[0].astype(jnp.bfloat16)
    grad_up_b = jnp.sum(grad_pre.astype(jnp.float32), axis=0)
    grad_up_w = jnp.einsum("rd,rf->df", normed_two, grad_pre, preferred_element_type=jnp.float32)
    grad_normed_two = jnp.einsum("rf,df->rd", grad_pre, up_back, preferred_element_type=jnp.float32)
    norm_out, norm_back = jax.vjp(layer_norm, after, gain_two_f)
    grad_after_ln, grad_gain_two = norm_back(grad_normed_two)
    grad_after = grad_out + grad_after_ln
    grad_one = grad_after.astype(jnp.bfloat16)
    grad_out_w = jnp.einsum("rd,re->de", mixed_low, grad_one, preferred_element_type=jnp.float32)
    grad_mixed = jnp.einsum(
        "re,de->rd", grad_one, out_back, preferred_element_type=jnp.float32
    ).astype(jnp.bfloat16)
    back_keys, back_values = (
        lax.all_gather(key_low[:rows_dev], "leaf", axis=0, tiled=True),
        lax.all_gather(value_low[:rows_dev], "leaf", axis=0, tiled=True),
    )
    keys_back = jnp.concatenate([back_keys, key_low[rows_dev:]], axis=0)
    values_back = jnp.concatenate([back_values, value_low[rows_dev:]], axis=0)

    def head_backward(operands):
        q_head, k_head, v_head, g_head, norm_head = operands
        raw = jnp.einsum("qd,kd->qk", q_head, k_head, preferred_element_type=jnp.float32) * 0.125
        scores = jnp.where(mask_all, raw, NEG_FILL)
        probs = jnp.exp(scores - norm_head)
        grad_v = jnp.einsum(
            "qk,qd->kd", probs.astype(jnp.bfloat16), g_head, preferred_element_type=jnp.float32
        )
        grad_p = jnp.einsum("qd,kd->qk", g_head, v_head, preferred_element_type=jnp.float32)
        inner = jnp.sum(probs * grad_p, axis=-1, keepdims=True)
        grad_s = (probs * (grad_p - inner)).astype(jnp.bfloat16)
        grad_q = jnp.einsum("qk,kd->qd", grad_s, k_head, preferred_element_type=jnp.float32) * 0.125
        grad_k = jnp.einsum("qk,qd->kd", grad_s, q_head, preferred_element_type=jnp.float32) * 0.125
        return (grad_q, grad_k, grad_v)

    grad_q_heads, grad_k_heads, grad_v_heads = lax.map(
        head_backward,
        (
            q_heads,
            to_heads(keys_back, heads),
            to_heads(values_back, heads),
            to_heads(grad_mixed, heads),
            log_norm,
        ),
    )
    grad_query = from_heads(grad_q_heads)
    grad_keys_all = from_heads(grad_k_heads)
    grad_values_all = from_heads(grad_v_heads)
    own_key_grad, own_value_grad = (
        lax.psum_scatter(
            grad_keys_all[:tree_tok].astype(jnp.bfloat16), "leaf", scatter_dimension=0, tiled=True
        ).astype(jnp.float32),
        lax.psum_scatter(
            grad_values_all[:tree_tok].astype(jnp.bfloat16), "leaf", scatter_dimension=0, tiled=True
        ).astype(jnp.float32),
    )
    grad_key = jnp.concatenate([own_key_grad, grad_keys_all[tree_tok:]], axis=0)
    grad_value = jnp.concatenate([own_value_grad, grad_values_all[tree_tok:]], axis=0)
    grad_query = rotate(grad_query.reshape(2 * rows_dev, heads, HEAD_DIM), cosine, -sine).reshape(
        2 * rows_dev, width
    )
    grad_key = rotate(grad_key.reshape(2 * rows_dev, heads, HEAD_DIM), cosine, -sine).reshape(
        2 * rows_dev, width
    )
    grad_proj = jnp.concatenate([grad_query, grad_key, grad_value], axis=1).astype(jnp.bfloat16)
    grad_qkv_w = jnp.einsum("rd,re->de", normed_one, grad_proj, preferred_element_type=jnp.float32)
    grad_normed_one = jnp.einsum(
        "re,de->rd", grad_proj, qkv_back, preferred_element_type=jnp.float32
    )
    first_out, first_back = jax.vjp(layer_norm, stream, gain_one_f)
    grad_stream_ln, grad_gain_one = first_back(grad_normed_one)
    grad_stream = grad_after + grad_stream_ln
    grad_clean = grad_stream[:rows_dev] + jnp.where(masked, 0.0, grad_stream[rows_dev:])
    grad_embed = jnp.sum(jnp.where(masked, grad_stream[rows_dev:], 0.0), axis=0)
    summed = (
        lax.psum_scatter(grad_gain_one, ("leaf", "fsdp"), scatter_dimension=0, tiled=True),
        lax.psum_scatter(grad_qkv_w, ("leaf", "fsdp"), scatter_dimension=0, tiled=True),
        lax.psum_scatter(grad_out_w, ("leaf", "fsdp"), scatter_dimension=0, tiled=True),
        lax.psum_scatter(grad_gain_two, ("leaf", "fsdp"), scatter_dimension=0, tiled=True),
        lax.psum_scatter(grad_up_w, ("leaf", "fsdp"), scatter_dimension=0, tiled=True),
        lax.psum_scatter(grad_up_b, ("leaf", "fsdp"), scatter_dimension=0, tiled=True),
        lax.psum_scatter(grad_down_w, ("leaf", "fsdp"), scatter_dimension=0, tiled=True),
        lax.psum_scatter(grad_down_b, ("leaf", "fsdp"), scatter_dimension=0, tiled=True),
        lax.psum_scatter(grad_embed, ("leaf", "fsdp"), scatter_dimension=0, tiled=True),
    )
    return (
        output,
        grad_clean.astype(jnp.bfloat16)[None],
        summed[0],
        summed[1],
        summed[2],
        summed[3],
        summed[4],
        summed[5],
        summed[6],
        summed[7],
        summed[8],
    )


def solution(mesh):
    in_specs = (
        P("fsdp", "leaf", None),
        P("fsdp", "leaf"),
        P("fsdp", None),
        P("fsdp", None),
        P(("leaf", "fsdp")),
        P(("leaf", "fsdp"), None),
        P(("leaf", "fsdp"), None),
        P(("leaf", "fsdp")),
        P(("leaf", "fsdp"), None),
        P(("leaf", "fsdp")),
        P(("leaf", "fsdp"), None),
        P(("leaf", "fsdp")),
        P(("leaf", "fsdp")),
        P("fsdp", None, "leaf", None),
    )
    out_specs = (
        P("fsdp", None, "leaf", None),
        P("fsdp", "leaf", None),
        P(("leaf", "fsdp")),
        P(("leaf", "fsdp"), None),
        P(("leaf", "fsdp"), None),
        P(("leaf", "fsdp")),
        P(("leaf", "fsdp"), None),
        P(("leaf", "fsdp")),
        P(("leaf", "fsdp"), None),
        P(("leaf", "fsdp")),
        P(("leaf", "fsdp")),
    )
    return jax.shard_map(shards, mesh=mesh, in_specs=in_specs, out_specs=out_specs, check_vma=False)
```

profile of v0, /device:TPU:0, one launch (start us, length us, event | category | flops | bytes accessed | tf_op | source)
XLA Modules:
  0.0 1240.7 jit_solution(11994550310879820292)
XLA Ops:
  12.2 42.3 %all-reduce.12 = (bf16[768]{0:T(1024)(128)(2,1)S(1)}, bf16[768]{0:T(1024)(128)(2,1)S(1)}, bf16[768]{0:T(1024)(128)(2,1)}, bf16[768]{0:T(1024)(128)(2,1)S(1)}, bf16[3072]{0:T(1024)(128)(2,1)S(1)}) all-reduce(bf16[768]{0:T(1024)(128)(2,1)S(1)} %dynamic-update-slice.1, ...), channel_id=1, replica_groups=mesh['leaf'=8,'fsdp'=4] {'leaf','fsdp'}, use_global_device_ids=true, to_apply=%add.2 | all-reduce | flops 6144 | bytes 24576
  58.5 15.2 %all-gather.7.cloned.1.call-done = bf16[768,2304]{1,0:T(8,128)(2,1)} async-done(((bf16[24,2304]{1,0:T(8,128)(2,1)}), bf16[768,2304]{1,0:T(8,128)(2,1)}) %all-gather.7.cloned.1.call-update) | async-done | bytes 3538960 | tf_op jit(solution)/shard_map/all_gather | solution.py:77
  73.8 6.2 fusion.73
  83.0 3.9 fusion.71
  88.9 3.0 copy.76
  91.9 2.7 subtract_convert_fusion.2
  105.6 34.7 %all-gather.11.cloned.1.call-done = bf16[2048,768]{1,0:T(8,128)(2,1)} async-done(((bf16[256,768]{1,0:T(8,128)(2,1)}), bf16[2048,768]{1,0:T(8,128)(2,1)}) %all-gather.11.cloned.1.call-update) | async-done | bytes 3145744 | tf_op jit(solution)/shard_map/all_gather | solution.py:145
  140.3 4.0 pad_maximum_fusion.1
  144.3 5.9 copy.80
  150.2 53.8 %all-gather.9.cloned.1.call-done = bf16[2048,768]{0,1:T(8,128)(2,1)} async-done(((bf16[256,768]{0,1:T(8,128)(2,1)}), bf16[2048,768]{0,1:T(8,128)(2,1)}) %all-gather.9.cloned.1.call-update) | async-done | bytes 3145744 | tf_op jit(solution)/shard_map/all_gather | solution.py:144
  204.1 4.0 pad_maximum_fusion
  208.1 7.9 copy.82
  216.0 8.0 copy.84
  224.0 69.5 %while.28 = (s32[]{:T(128)}, bf16[12,512,64]{1,2,0:T(8,128)(2,1)S(1)}, f32[12,512,1]{1,2,0:T(1,128)}, bf16[12,512,64]{2,1,0:T(8,128)(2,1)}, bf16[12,2304,64]{2,1...) while((s32[]{:T(128)}, ...), condition=%wide.region_14.15_spmd.clone, body=%wide.region_11.14_spmd.sunk.clone | while | flops 311426560 | bytes 16799832 | solution.py:165
  297.5 27.0 %all-gather.15.cloned.1.call-done = bf16[768,3072]{1,0:T(8,128)(2,1)} async-done(((bf16[24,3072]{1,0:T(8,128)(2,1)}), bf16[768,3072]{1,0:T(8,128)(2,1)}) %all-gather.15.cloned.1.call-update) | async-done | bytes 4718608 | tf_op jit(solution)/shard_map/all_gather | solution.py:80
  324.5 8.2 fusion.64
  332.7 57.0 %all-gather.17.cloned.1.call-done = bf16[3072,768]{1,0:T(8,128)(2,1)} async-done(((bf16[96,768]{1,0:T(8,128)(2,1)}), bf16[3072,768]{1,0:T(8,128)(2,1)}) %all-gather.17.cloned.1.call-update) | async-done | bytes 4718608 | tf_op jit(solution)/shard_map/all_gather | solution.py:82
  389.7 9.9 convert_reduce_fusion
  399.6 3.4 multiply_reduce_fusion.1
  410.1 154.7 %while.29 = (s32[]{:T(128)}, f32[12,512,64]{1,2,0:T(8,128)}, f32[12,2304,64]{1,2,0:T(8,128)}, bf16[12,2304,64]{1,2,0:T(8,128)(2,1)}, bf16[12,512,64]{2,1,0:T(8,1...) while((s32[]{:T(128)}, f32[12,512,64]{1,2,0:T(8,128)}, ...), condition=%wide.region_21.22_spmd.clone, body=%wide.region_19.21_spmd.sunk.clone | while | flops 765771264 | bytes 40057968 | solution.py:238
  412.7 2.8 multiply_reduce_fusion.9
  425.5 2.8 multiply_reduce_fusion.9
  438.4 2.8 multiply_reduce_fusion.9
  451.3 2.8 multiply_reduce_fusion.9
  464.2 2.8 multiply_reduce_fusion.9
  469.6 2.6 fusion.139
  477.0 2.8 multiply_reduce_fusion.9
  489.9 2.8 multiply_reduce_fusion.9
  502.8 2.8 multiply_reduce_fusion.9
  515.7 2.8 multiply_reduce_fusion.9
  528.6 2.8 multiply_reduce_fusion.9
  541.5 2.8 multiply_reduce_fusion.9
  554.4 2.8 multiply_reduce_fusion.9
  559.8 2.6 fusion.139
  564.7 4.9 slice.169
  569.7 3.9 slice.123
  574.8 3.5 fusion.75
  578.3 10.1 fusion.66
  589.9 7.2 fusion.63
  601.2 42.4 %reduce-scatter.7.cloned.1.call-done = bf16[256,768]{0,1:T(8,128)(2,1)} async-done(((bf16[2048,768]{0,1:T(8,128)(2,1)}), bf16[256,768]{0,1:T(8,128)(2,1)}) %reduce-scatter.7.cloned.1.call-update) | async-done | bytes 393232 | tf_op jit(solution)/shard_map/reduce_scatter | solution.py:252
  648.9 72.4 %reduce-scatter.9.cloned.1.call-done = bf16[256,768]{0,1:T(8,128)(2,1)} async-done(((bf16[2048,768]{0,1:T(8,128)(2,1)}), bf16[256,768]{0,1:T(8,128)(2,1)}) %reduce-scatter.9.cloned.1.call-update) | async-done | bytes 393232 | tf_op jit(solution)/shard_map/reduce_scatter | solution.py:255
  721.3 6.7 fusion.52
  730.6 9.3 add_convert_fusion
  745.6 40.2 %all-reduce.11 = (f32[768]{0:T(1024)S(1)}, f32[768]{0:T(1024)S(1)}, f32[3072]{0:T(1024)S(1)}, f32[768]{0:T(1024)S(1)}, f32[768]{0:T(1024)S(1)}) all-reduce(f32[768]{0:T(1024)S(1)} %get-tuple-element.195, f32[768]{0:T(1024)S(1)} %copy-done.34, f32[3072]{0:T(1024)S(1)} %copy-done.31, ...), channel_id=4, replica_groups=mesh['leaf'=8,'fsdp'=4] {'leaf','fsdp'}, use_global_device_ids=true, to_apply=%region_27.28.clone | all-reduce | flops 6144 | bytes 49152
  788.8 36.7 %reduce-scatter.13.cloned.1.call-done = f32[24,768]{1,0:T(8,128)} async-done(((f32[768,768]{1,0:T(8,128)}), f32[24,768]{1,0:T(8,128)}) %reduce-scatter.13.cloned.1.call-update) | async-done | bytes 73744 | tf_op jit(solution)/shard_map/reduce_scatter | solution.py:280
  825.5 141.8 %reduce-scatter.17.cloned.1.call-done = f32[96,768]{1,0:T(8,128)} async-done(((f32[3072,768]{1,0:T(8,128)}), f32[96,768]{1,0:T(8,128)}) %reduce-scatter.17.cloned.1.call-update) | async-done | bytes 294928 | tf_op jit(solution)/shard_map/reduce_scatter | solution.py:284
  967.3 141.1 %reduce-scatter.15.cloned.1.call-done = f32[24,3072]{1,0:T(8,128)} async-done(((f32[768,3072]{1,0:T(8,128)}), f32[24,3072]{1,0:T(8,128)}) %reduce-scatter.15.cloned.1.call-update) | async-done | bytes 294928 | tf_op jit(solution)/shard_map/reduce_scatter | solution.py:282
  1108.4 125.2 %reduce-scatter.11.cloned.1.call-done = f32[24,2304]{1,0:T(8,128)} async-done(((f32[768,2304]{1,0:T(8,128)}), f32[24,2304]{1,0:T(8,128)}) %reduce-scatter.11.cloned.1.call-update) | async-done | bytes 221200 | tf_op jit(solution)/shard_map/reduce_scatter | solution.py:279
  (324 shorter events, 243.5 us)
Async XLA Ops:
  7.2 66.6 %all-gather.7.cloned.1.call-start = ((), (), s32[]{:S(2)}) async-start(), calls=%async_computation.6 | async-start | bytes 3649536 | tf_op jit(solution)/shard_map/all_gather | solution.py:77
  7.9 132.4 %all-gather.11.cloned.1.call-start = ((), (), s32[]{:S(2)}) async-start(), calls=%async_computation.8 | async-start | bytes 3538944 | tf_op jit(solution)/shard_map/all_gather | solution.py:145
  54.5 19.2 %copy-start.26 = (f32[768]{0:T(1024)}, f32[768]{0:T(1024)S(1)}, u32[]{:S(2)}) copy-start(f32[768]{0:T(1024)S(1)} %convert_element_type.105) | copy-start | bytes 9220
  55.2 2.7 copy-start.35
  57.6 22.4 %copy-start.22 = (f32[512]{0:T(512)}, f32[512]{0:T(512)S(1)}, u32[]{:S(2)}) copy-start(f32[512]{0:T(512)S(1)} %broadcast_multiply_fusion.1) | copy-start | bytes 6148
  58.5 21.5 %copy-start.24 = (f32[512]{0:T(512)}, f32[512]{0:T(512)S(1)}, u32[]{:S(2)}) copy-start(f32[512]{0:T(512)S(1)} %fusion.57) | copy-start | bytes 6148
  58.5 22.5 %copy-start.37 = (s32[1,128]{1,0:T(1,128)S(1)}, s32[1,128]{1,0:T(1,128)}, u32[]{:S(2)}) copy-start(s32[1,128]{1,0:T(1,128)} %param.20) | copy-start | bytes 1540
  58.5 22.8 %copy-start.33 = (s32[1,13]{1,0:T(1,128)S(1)}, s32[1,13]{1,0:T(1,128)}, u32[]{:S(2)}) copy-start(s32[1,13]{1,0:T(1,128)} %param.21) | copy-start | bytes 160
  81.0 123.1 %all-gather.9.cloned.1.call-start = ((), (), s32[]{:S(2)}) async-start(), calls=%async_computation.7 | async-start | bytes 3538944 | tf_op jit(solution)/shard_map/all_gather | solution.py:144
  83.0 8.9 copy-start.18
  95.6 197.8 %all-gather.13.cloned.1.call-start = ((), (), s32[]{:S(2)}) async-start(), calls=%async_computation.9 | async-start | bytes 1216512 | tf_op jit(solution)/shard_map/all_gather | solution.py:78
  96.2 228.2 %all-gather.15.cloned.1.call-start = ((), (), s32[]{:S(2)}) async-start(), calls=%async_computation.10 | async-start | bytes 4866048 | tf_op jit(solution)/shard_map/all_gather | solution.py:80
  96.8 292.9 %all-gather.17.cloned.1.call-start = ((), (), s32[]{:S(2)}) async-start(), calls=%async_computation.11 | async-start | bytes 4866048 | tf_op jit(solution)/shard_map/all_gather | solution.py:82
  97.4 546.2 %reduce-scatter.7.cloned.1.call-start = ((), (), s32[]{:S(2)}) async-start(), calls=%async_computation.12 | async-start | bytes 3538944 | tf_op jit(solution)/shard_map/reduce_scatter | solution.py:252
  100.4 3.5 copy-start.14
  100.5 3.5 copy-start.15
  144.3 59.8 %copy-start.13 = (bf16[256,12,64]{0,2,1:T(8,128)(2,1)S(1)}, bf16[256,12,64]{0,2,1:T(8,128)(2,1)}, u32[]{:S(2)}) copy-start(bf16[256,12,64]{0,2,1:T(8,128)(2,1)} %get-tuple-element.274) | copy-start | bytes 1179652
  216.0 8.0 copy-start.8
  293.4 2.5 copy-start.9
  295.9 1.2 copy-start.2
  297.4 92.3 %copy-start.5 = (bf16[1,2,256,768]{3,2,1,0:T(8,128)(2,1)S(1)}, bf16[1,2,256,768]{3,2,1,0:T(8,128)(2,1)}, u32[]{:S(2)}) copy-start(bf16[1,2,256,768]{3,2,1,0:T(8,128)(2,1)} %param.31) | copy-start | bytes 2359300
  389.7 9.9 copy-start.3
  389.7 9.9 copy-start.38
  399.6 3.4 copy-start.12
  403.7 2.3 copy-start.39
  569.7 151.7 %reduce-scatter.9.cloned.1.call-start = ((), (), s32[]{:S(2)}) async-start(), calls=%async_computation.13 | async-start | bytes 3538944 | tf_op jit(solution)/shard_map/reduce_scatter | solution.py:255
  573.7 4.6 copy-start.32
  573.7 251.8 %reduce-scatter.13.cloned.1.call-start = ((), (), s32[]{:S(2)}) async-start(), calls=%async_computation.15 | async-start | bytes 2433024 | tf_op jit(solution)/shard_map/reduce_scatter | solution.py:280
  578.3 389.1 %reduce-scatter.17.cloned.1.call-start = ((), (), s32[]{:S(2)}) async-start(), calls=%async_computation.17 | async-start | bytes 9732096 | tf_op jit(solution)/shard_map/reduce_scatter | solution.py:284
  588.4 1.4 copy-start.4
  588.5 520.0 %reduce-scatter.15.cloned.1.call-start = ((), (), s32[]{:S(2)}) async-start(), calls=%async_computation.16 | async-start | bytes 9732096 | tf_op jit(solution)/shard_map/reduce_scatter | solution.py:282
  597.0 47.6 %copy-start.19 = (f32[512,32]{0,1:T(8,128)S(1)}, f32[512,32]{0,1:T(8,128)}, u32[]{:S(2)}) copy-start(f32[512,32]{0,1:T(8,128)} %copy-done.18) | copy-start | bytes 196612
  597.1 47.6 %copy-start.21 = (f32[512,32]{0,1:T(8,128)S(1)}, f32[512,32]{0,1:T(8,128)}, u32[]{:S(2)}) copy-start(f32[512,32]{0,1:T(8,128)} %get-tuple-element.281) | copy-start | bytes 196612
  597.1 636.5 %reduce-scatter.11.cloned.1.call-start = ((), (), s32[]{:S(2)}) async-start(), calls=%async_computation.14 | async-start | bytes 7299072 | tf_op jit(solution)/shard_map/reduce_scatter | solution.py:279
  646.9 74.4 %copy-start.20 = (bf16[256,12,64]{0,2,1:T(8,128)(2,1)S(1)}, bf16[256,12,64]{0,2,1:T(8,128)(2,1)}, u32[]{:S(2)}) copy-start(bf16[256,12,64]{0,2,1:T(8,128)(2,1)} %slice.124) | copy-start | bytes 1179652
  646.9 74.4 %copy-start.23 = (f32[512]{0:T(512)S(1)}, f32[512]{0:T(512)}, u32[]{:S(2)}) copy-start(f32[512]{0:T(512)} %copy-done.22) | copy-start | bytes 6148
  647.0 74.4 %copy-start.25 = (f32[512]{0:T(512)S(1)}, f32[512]{0:T(512)}, u32[]{:S(2)}) copy-start(f32[512]{0:T(512)} %copy-done.24) | copy-start | bytes 6148
  647.0 74.4 %copy-start.27 = (f32[768]{0:T(1024)S(1)}, f32[768]{0:T(1024)}, u32[]{:S(2)}) copy-start(f32[768]{0:T(1024)} %copy-done.26) | copy-start | bytes 9220
  730.6 9.3 copy-start.7
  730.6 9.3 copy-start.16
  730.6 9.3 copy-start.17
  730.6 9.3 copy-start.40
  739.9 2.5 copy-start.29
  742.4 1.4 copy-start.1
  742.4 1.6 copy-start.6
  744.0 1.6 copy-start.30
  744.0 1.6 copy-start.31
  744.0 1.6 copy-start.34
  (5 other events, 4.4 us)
Sparse Core Ops, SparseCore 0:
  10.9 62.7 all-gather.6
  81.1 59.1 all-gather.10
  142.3 61.6 all-gather.8
  206.8 52.2 all-gather.12
  261.9 62.5 all-gather.14
  327.2 62.4 all-gather.16
  569.8 73.7 reduce-scatter.6
  647.2 74.0 reduce-scatter.8
  727.2 98.2 reduce-scatter.12
  832.8 134.4 reduce-scatter.16
  973.8 134.5 reduce-scatter.14
  1115.5 118.0 reduce-scatter.10
where the time goes:
time: 1250 us; the launch traced here: 1240 us
  waiting for transfers between devices  750 us (60%)
  matrix products  264 us (21%)
  blocking collectives  82.6 us (7%)
  local copies, waits for them, and re-layouts  80.2 us (6%)
  other arithmetic  47 us (4%)
  between operations  15 us (1%)
    reduce_scatter x1, waiting for transfers between devices, shards(): lax.psum_scatter(grad_down_w, ('leaf', 'fsdp'), scatter_dimension=0, tile...  142 us
    reduce_scatter x1, waiting for transfers between devices, shards(): lax.psum_scatter(grad_up_w, ('leaf', 'fsdp'), scatter_dimension=0, tiled=...  141 us
    reduce_scatter x1, waiting for transfers between devices, shards(): lax.psum_scatter(grad_qkv_w, ('leaf', 'fsdp'), scatter_dimension=0, tiled...  125 us
    unnamed x2, blocking collectives  82.6 us
    reduce_scatter x1, waiting for transfers between devices, shards(): lax.psum_scatter(grad_values_all[:tree_tok].astype(jnp.bfloat16), 'leaf',...  72.4 us
    all_gather x1, waiting for transfers between devices, shards(): lax.all_gather(w_down, ('leaf', 'fsdp'), axis=0, tiled=True)  57 us
    all_gather x1, waiting for transfers between devices, shards(): lax.all_gather(key_low[:rows_dev], 'leaf', axis=0, tiled=True)  53.8 us
    reduce_scatter x1, waiting for transfers between devices, shards(): lax.psum_scatter(grad_keys_all[:tree_tok].astype(jnp.bfloat16), 'leaf', s...  42.4 us
  transfers between devices with their start and end apart: 12, of which 11 were waited for; matrix products, arithmetic and copies ran while one was open for 16% of the time, Pallas kernels for 0%

commit v1 on v0

--- a/solution.py
+++ b/solution.py
@@ -1,13 +1,39 @@
+import functools
 import math
 import jax
 import jax.numpy as jnp
 from jax import lax
 from jax.sharding import PartitionSpec as P
+from jax.lax import axis_index, axis_size, ppermute
 
 HEAD_DIM = 64
 BLOCK = 16
 NEG_FILL = -1000000000.0
 EPSILON = 1e-05
+
+
+def make_the_tails(x_in, axis_no):
+    current_arr = axis_index("leaf")
+    t1 = axis_size("leaf")
+    carry_out, h_now, local_next = (t1, current_arr, x_in.shape[axis_no])
+    in_order = [k0 * carry_out if j0 == axis_no else k0 for j0, k0 in enumerate(x_in.shape)]
+    mid_arr = jnp.zeros(in_order, x_in.dtype)
+    earlier = r2 = x_in
+    f_next = lax.dynamic_update_slice_in_dim(mid_arr, x_in, h_now * local_next, axis=axis_no)
+    for s in range(1, carry_out // 2 + 1):
+        earlier = ppermute(earlier, "leaf", [(j0, (j0 + 1) % carry_out) for j0 in range(carry_out)])
+        f_next = lax.dynamic_update_slice_in_dim(
+            f_next, earlier, (h_now - s) % carry_out * local_next, axis=axis_no
+        )
+        if 2 * s < carry_out:
+            r2 = ppermute(r2, "leaf", [(j0, (j0 - 1) % carry_out) for j0 in range(carry_out)])
+            f_next = lax.dynamic_update_slice_in_dim(
+                f_next, r2, (h_now + s) % carry_out * local_next, axis=axis_no
+            )
+    return f_next
+
+
+remake_slabs = functools.partial(make_the_tails, axis_no=0)
 
 
 def look_up(table, indices):
@@ -142,7 +168,7 @@
     value_low = projected[:, 2 * width :].astype(jnp.bfloat16)
     tree_keys, tree_values = (
         lax.all_gather(key_low[:rows_dev], "leaf", axis=0, tiled=True),
-        lax.all_gather(value_low[:rows_dev], "leaf", axis=0, tiled=True),
+        remake_slabs(value_low[:rows_dev]),
     )
     tree_tok = tree_keys.shape[0]
     keys_all = jnp.concatenate([tree_keys, key_low[rows_dev:]], axis=0)

time: 1250 us -> 1310 us (1.048)
  matrix products: 264 us -> 278 us
  starting transfers between devices: 1.16 us -> 15 us
  local copies, waits for them, and re-layouts: 80.2 us -> 93.4 us
    all_gather x1, waiting for transfers between devices: 53.8 us -> 1.52 us  [shards(): lax.all_gather(key_low[:rows_dev], 'leaf', axis=0, tiled=True)]
    ppermute x0 -> x7, waiting for transfers between devices: none -> 47.1 us  [the longest x3 34.2 us: make_the_tails(): ppermute(r2, 'leaf', [(j0, (j0 - 1) % carry_out) for j0 in range(carry_ou...]
    all_gather x1, waiting for transfers between devices: 34.7 us -> 0.01 us  [shards(): lax.all_gather(value_low[:rows_dev], 'leaf', axis=0, tiled=True)]
    all_gather x1, waiting for transfers between devices: 27 us -> 61.7 us  [shards(): lax.all_gather(w_up, ('leaf', 'fsdp'), axis=0, tiled=True)]
    all_gather x1, waiting for transfers between devices: 0.01 us -> 19.3 us  [shards(): lax.all_gather(w_out, ('leaf', 'fsdp'), axis=0, tiled=True)]
    ppermute x0 -> x7, starting transfers between devices: none -> 14.3 us  [the longest x3 7.77 us: make_the_tails(): ppermute(r2, 'leaf', [(j0, (j0 - 1) % carry_out) for j0 in range(carry_ou...]
  transfers between devices with their start and end apart: 12 -> 19, of which waited for: 11 -> 15; matrix products, arithmetic and copies ran while one was open for 16% -> 17% of each run, Pallas kernels for 0% -> 0%
where the time goes in v1:
time: 1310 us; the launch traced here: 1300 us
  waiting for transfers between devices  759 us (58%)
  matrix products  278 us (21%)
  local copies, waits for them, and re-layouts  93.4 us (7%)
  blocking collectives  82.6 us (6%)
  other arithmetic  57.3 us (4%)
  between operations  15.2 us (1%)
  starting transfers between devices  15 us (1%)
    reduce_scatter x1, waiting for transfers between devices, shards(): lax.psum_scatter(grad_down_w, ('leaf', 'fsdp'), scatter_dimension=0, tile...  142 us
    reduce_scatter x1, waiting for transfers between devices, shards(): lax.psum_scatter(grad_up_w, ('leaf', 'fsdp'), scatter_dimension=0, tiled=...  141 us
    reduce_scatter x1, waiting for transfers between devices, shards(): lax.psum_scatter(grad_qkv_w, ('leaf', 'fsdp'), scatter_dimension=0, tiled...  126 us
    unnamed x2, blocking collectives  82.6 us
    reduce_scatter x1, waiting for transfers between devices, shards(): lax.psum_scatter(grad_values_all[:tree_tok].astype(jnp.bfloat16), 'leaf',...  72.3 us
    all_gather x1, waiting for transfers between devices, shards(): lax.all_gather(w_up, ('leaf', 'fsdp'), axis=0, tiled=True)  61.7 us
    all_gather x1, waiting for transfers between devices, shards(): lax.all_gather(w_down, ('leaf', 'fsdp'), axis=0, tiled=True)  57 us
    reduce_scatter x1, waiting for transfers between devices, shards(): lax.psum_scatter(grad_keys_all[:tree_tok].astype(jnp.bfloat16), 'leaf', s...  42.5 us
  transfers between devices with their start and end apart: 19, of which 15 were waited for; matrix products, arithmetic and copies ran while one was open for 17% of the time, Pallas kernels for 0%

profile of v1, /device:TPU:0, one launch (start us, length us, event | category | flops | bytes accessed | tf_op | source)
XLA Modules:
  0.0 1300.5 jit_solution(17583258657728697384)
XLA Ops:
  13.1 42.4 %all-reduce.12 = (bf16[768]{0:T(1024)(128)(2,1)S(1)}, bf16[768]{0:T(1024)(128)(2,1)S(1)}, bf16[768]{0:T(1024)(128)(2,1)}, bf16[768]{0:T(1024)(128)(2,1)S(1)}, bf16[3072]{0:T(1024)(128)(2,1)S(1)}) all-reduce(bf16[768]{0:T(1024)(128)(2,1)S(1)} %dynamic-update-slice.1, ...), channel_id=1, replica_groups=mesh['leaf'=8,'fsdp'=4] {'leaf','fsdp'}, use_global_device_ids=true, to_apply=%add.2 | all-reduce | flops 6144 | bytes 24576
  63.9 9.9 all-gather.7.cloned.1.call-done
  73.8 5.5 fusion.74
  83.0 3.0 copy.103
  93.9 3.0 collective-permute-start.1
  97.4 20.7 %collective-permute-done.1 = bf16[256,768]{1,0:T(8,128)(2,1)} collective-permute-done((bf16[256,768]{1,0:T(8,128)(2,1)}, bf16[256,768]{1,0:T(8,128)(2,1)}, u32[]{:S(2)}, u32[]{:S(2)}) %collective-permute-start.1) | collective-permute-done | bytes 393248 | tf_op jit(solution)/shard_map/ppermute | solution.py:29
  120.8 3.0 pad_add_fusion
  127.9 10.2 collective-permute-done.2
  150.0 3.6 collective-permute-start.5
  160.3 3.9 collective-permute-start.6
  168.2 13.5 %collective-permute-done.5 = bf16[256,768]{1,0:T(8,128)(2,1)} collective-permute-done((bf16[256,768]{1,0:T(8,128)(2,1)}, bf16[256,768]{1,0:T(8,128)(2,1)}, u32[]{:S(2)}, u32[]{:S(2)}) %collective-permute-start.5) | collective-permute-done | bytes 393248 | tf_op jit(solution)/shard_map/ppermute | solution.py:29
  188.2 4.1 pad_maximum_fusion.1
  193.9 4.0 pad_maximum_fusion
  197.9 8.0 copy.117
  205.9 75.5 %while.28 = (s32[]{:T(128)}, bf16[12,512,64]{1,2,0:T(8,128)(2,1)}, f32[12,512,1]{1,2,0:T(1,128)}, bf16[12,512,64]{2,1,0:T(8,128)(2,1)}, bf16[12,2304,64]{2,1,0:T...) while((s32[]{:T(128)}, bf16[12,512,64]{1,2,0:T(8,128)(2,1)}, ...), condition=%wide.region_14.15_spmd.clone, body=%wide.region_11.14_spmd.sunk.clone | while | flops 311426560 | bytes 16504921 | solution.py:191
  281.3 3.9 pad_maximum_fusion.2
  285.2 5.9 copy.121
  291.1 19.3 %all-gather.11.cloned.1.call-done = bf16[768,768]{1,0:T(8,128)(2,1)} async-done(((bf16[24,768]{1,0:T(8,128)(2,1)}), bf16[768,768]{1,0:T(8,128)(2,1)}) %all-gather.11.cloned.1.call-update) | async-done | bytes 1179664 | tf_op jit(solution)/shard_map/all_gather | solution.py:104
  314.0 61.7 %all-gather.13.cloned.1.call-done = bf16[768,3072]{1,0:T(8,128)(2,1)} async-done(((bf16[24,3072]{1,0:T(8,128)(2,1)}), bf16[768,3072]{1,0:T(8,128)(2,1)}) %all-gather.13.cloned.1.call-update) | async-done | bytes 4718608 | tf_op jit(solution)/shard_map/all_gather | solution.py:106
  375.7 8.2 fusion.65
  384.0 57.0 %all-gather.15.cloned.1.call-done = bf16[3072,768]{1,0:T(8,128)(2,1)} async-done(((bf16[96,768]{1,0:T(8,128)(2,1)}), bf16[3072,768]{1,0:T(8,128)(2,1)}) %all-gather.15.cloned.1.call-update) | async-done | bytes 4718608 | tf_op jit(solution)/shard_map/all_gather | solution.py:108
  441.0 19.8 %convert_reduce_fusion = (f32[3072]{0:T(1024)}, bf16[512,3072]{1,0:T(8,128)(2,1)S(1)}) fusion(f32[512,3072]{1,0:T(8,128)} %fusion.65, f32[3072]{0:T(1024)} %convert_element_type.115, bf16[512,768]{1,0:T(8,128)(2,1)S(1)} %bitcast.189, bf16[3072,768]{1,0:T(8,128)(2,1)} %all-gather.15.cloned.1.call-done), kind=kOutput, calls=%fused_computation.64 | convolution fusion | flops 2452091904 | bytes 14966784 | tf_op jit(solution)/shard_map/rd,fd->rf/dot_general | solution.py:228
  460.8 3.4 multiply_reduce_fusion.1
  471.3 152.9 %while.29 = (s32[]{:T(128)}, f32[12,512,64]{1,2,0:T(8,128)}, f32[12,2304,64]{1,2,0:T(8,128)}, bf16[12,2304,64]{1,2,0:T(8,128)(2,1)}, bf16[12,512,64]{2,1,0:T(8,1...) while((s32[]{:T(128)}, f32[12,512,64]{1,2,0:T(8,128)}, ...), condition=%wide.region_21.22_spmd.clone, body=%wide.region_19.21_spmd.sunk.clone | while | flops 765771264 | bytes 39763056 | solution.py:264
  473.8 2.8 multiply_reduce_fusion.9
  486.6 2.8 multiply_reduce_fusion.9
  499.3 2.8 multiply_reduce_fusion.9
  512.0 2.8 multiply_reduce_fusion.9
  524.7 2.8 multiply_reduce_fusion.9
  537.5 2.8 multiply_reduce_fusion.9
  562.9 2.8 multiply_reduce_fusion.9
  588.4 2.8 multiply_reduce_fusion.9
  601.2 2.8 multiply_reduce_fusion.9
  614.0 2.8 multiply_reduce_fusion.9
  624.3 4.9 slice.169
  629.2 3.9 slice.123
  634.3 3.4 fusion.76
  637.8 10.0 fusion.67
  649.3 7.2 fusion.64
  660.6 42.5 %reduce-scatter.7.cloned.1.call-done = bf16[256,768]{0,1:T(8,128)(2,1)} async-done(((bf16[2048,768]{0,1:T(8,128)(2,1)}), bf16[256,768]{0,1:T(8,128)(2,1)}) %reduce-scatter.7.cloned.1.call-update) | async-done | bytes 393232 | tf_op jit(solution)/shard_map/reduce_scatter | solution.py:278
  708.4 72.3 %reduce-scatter.9.cloned.1.call-done = bf16[256,768]{0,1:T(8,128)(2,1)} async-done(((bf16[2048,768]{0,1:T(8,128)(2,1)}), bf16[256,768]{0,1:T(8,128)(2,1)}) %reduce-scatter.9.cloned.1.call-update) | async-done | bytes 393232 | tf_op jit(solution)/shard_map/reduce_scatter | solution.py:281
  780.8 6.7 fusion.52
  790.0 9.3 add_convert_fusion
  804.8 40.2 %all-reduce.11 = (f32[768]{0:T(1024)S(1)}, f32[768]{0:T(1024)S(1)}, f32[3072]{0:T(1024)S(1)}, f32[768]{0:T(1024)S(1)}, f32[768]{0:T(1024)S(1)}) all-reduce(f32[768]{0:T(1024)S(1)} %get-tuple-element.195, f32[768]{0:T(1024)S(1)} %copy-done.32, f32[3072]{0:T(1024)S(1)} %copy-done.30, ...), channel_id=4, replica_groups=mesh['leaf'=8,'fsdp'=4] {'leaf','fsdp'}, use_global_device_ids=true, to_apply=%region_27.28.clone | all-reduce | flops 6144 | bytes 49152
  848.0 36.9 %reduce-scatter.13.cloned.1.call-done = f32[24,768]{1,0:T(8,128)} async-done(((f32[768,768]{1,0:T(8,128)}), f32[24,768]{1,0:T(8,128)}) %reduce-scatter.13.cloned.1.call-update) | async-done | bytes 73744 | tf_op jit(solution)/shard_map/reduce_scatter | solution.py:306
  884.9 141.9 %reduce-scatter.17.cloned.1.call-done = f32[96,768]{1,0:T(8,128)} async-done(((f32[3072,768]{1,0:T(8,128)}), f32[96,768]{1,0:T(8,128)}) %reduce-scatter.17.cloned.1.call-update) | async-done | bytes 294928 | tf_op jit(solution)/shard_map/reduce_scatter | solution.py:310
  1026.7 141.0 %reduce-scatter.15.cloned.1.call-done = f32[24,3072]{1,0:T(8,128)} async-done(((f32[768,3072]{1,0:T(8,128)}), f32[24,3072]{1,0:T(8,128)}) %reduce-scatter.15.cloned.1.call-update) | async-done | bytes 294928 | tf_op jit(solution)/shard_map/reduce_scatter | solution.py:308
  1167.7 125.5 %reduce-scatter.11.cloned.1.call-done = f32[24,2304]{1,0:T(8,128)} async-done(((f32[768,2304]{1,0:T(8,128)}), f32[24,2304]{1,0:T(8,128)}) %reduce-scatter.11.cloned.1.call-update) | async-done | bytes 221200 | tf_op jit(solution)/shard_map/reduce_scatter | solution.py:305
  (352 shorter events, 297.0 us)
Async XLA Ops:
  7.2 66.6 %all-gather.7.cloned.1.call-start = ((), (), s32[]{:S(2)}) async-start(), calls=%async_computation.6 | async-start | bytes 3649536 | tf_op jit(solution)/shard_map/all_gather | solution.py:103
  7.9 186.0 %all-gather.9.cloned.1.call-start = ((), (), s32[]{:S(2)}) async-start(), calls=%async_computation.7 | async-start | bytes 3538944 | tf_op jit(solution)/shard_map/all_gather | solution.py:170
  55.5 23.8 %copy-start.25 = (f32[768]{0:T(1024)}, f32[768]{0:T(1024)S(1)}, u32[]{:S(2)}) copy-start(f32[768]{0:T(1024)S(1)} %convert_element_type.105) | copy-start | bytes 9220
  59.6 19.7 %copy-start.33 = (pred[256]{0:T(512)(128)(4,1)}, pred[256]{0:T(512)(128)(4,1)S(1)}, u32[]{:S(2)}) copy-start(pred[256]{0:T(512)(128)(4,1)S(1)} %compare_reduce_fusion) | copy-start | bytes 772
  62.0 17.3 %copy-start.21 = (f32[512]{0:T(512)}, f32[512]{0:T(512)S(1)}, u32[]{:S(2)}) copy-start(f32[512]{0:T(512)S(1)} %broadcast_multiply_fusion.1) | copy-start | bytes 6148
  62.9 16.4 %copy-start.23 = (f32[512]{0:T(512)}, f32[512]{0:T(512)S(1)}, u32[]{:S(2)}) copy-start(f32[512]{0:T(512)S(1)} %fusion.57) | copy-start | bytes 6148
  63.9 22.2 %copy-start.17 = (f32[512,32]{0,1:T(8,128)}, f32[512,32]{0,1:T(8,128)S(1)}, u32[]{:S(2)}) copy-start(f32[512,32]{0,1:T(8,128)S(1)} %get-tuple-element.283) | copy-start | bytes 196612
  88.8 4.8 copy-start.35
  89.8 191.5 %all-gather.17.cloned.1.call-start = ((), (), s32[]{:S(2)}) async-start(), calls=%async_computation.11 | async-start | bytes 3538944 | tf_op jit(solution)/shard_map/all_gather | solution.py:244
  91.8 218.6 %all-gather.11.cloned.1.call-start = ((), (), s32[]{:S(2)}) async-start(), calls=%async_computation.8 | async-start | bytes 1216512 | tf_op jit(solution)/shard_map/all_gather | solution.py:104
  92.4 283.3 %all-gather.13.cloned.1.call-start = ((), (), s32[]{:S(2)}) async-start(), calls=%async_computation.9 | async-start | bytes 4866048 | tf_op jit(solution)/shard_map/all_gather | solution.py:106
  93.0 348.0 %all-gather.15.cloned.1.call-start = ((), (), s32[]{:S(2)}) async-start(), calls=%async_computation.10 | async-start | bytes 4866048 | tf_op jit(solution)/shard_map/all_gather | solution.py:108
  93.6 609.5 %reduce-scatter.7.cloned.1.call-start = ((), (), s32[]{:S(2)}) async-start(), calls=%async_computation.12 | async-start | bytes 3538944 | tf_op jit(solution)/shard_map/reduce_scatter | solution.py:278
  93.9 24.2 %collective-permute-start.1 = (bf16[256,768]{1,0:T(8,128)(2,1)}, bf16[256,768]{1,0:T(8,128)(2,1)}, u32[]{:S(2)}, u32[]{:S(2)}) collective-permute-start(bf16[256,768]{1,0:T(8,128)(2,1)} %get-tuple-element.261), channel_id=1, source_target_pairs={{0,28},{4,0},{8,4},{12,8},{16,12},{20,16},{24,20},{28,24},{1,29},{... | collective-permute-start | bytes 1179656 | tf_op jit(solution)/shard_map/ppermute | solution.py:29
  96.9 22.3 %collective-permute-start = (bf16[256,768]{1,0:T(8,128)(2,1)}, bf16[256,768]{1,0:T(8,128)(2,1)}, u32[]{:S(2)}, u32[]{:S(2)}) collective-permute-start(bf16[256,768]{1,0:T(8,128)(2,1)} %get-tuple-element.261), channel_id=1, source_target_pairs={{0,4},{4,8},{8,12},{12,16},{16,20},{20,24},{24,28},{28,0},{1,5},{5... | collective-permute-start | bytes 1179656 | tf_op jit(solution)/shard_map/ppermute | solution.py:24
  118.1 31.9 %collective-permute-start.3 = (bf16[256,768]{1,0:T(8,128)(2,1)}, bf16[256,768]{1,0:T(8,128)(2,1)}, u32[]{:S(2)}, u32[]{:S(2)}) collective-permute-start(bf16[256,768]{1,0:T(8,128)(2,1)} %collective-permute-done.1), channel_id=1, source_target_pairs={{0,28},{4,0},{8,4},{12,8},{16,12},{20,16},{24,20},{28,24},{1,29},{... | collective-permute-start | bytes 1179656 | tf_op jit(solution)/shard_map/ppermute | solution.py:29
  119.2 18.8 %collective-permute-start.2 = (bf16[256,768]{1,0:T(8,128)(2,1)}, bf16[256,768]{1,0:T(8,128)(2,1)}, u32[]{:S(2)}, u32[]{:S(2)}) collective-permute-start(bf16[256,768]{1,0:T(8,128)(2,1)} %collective-permute-done), channel_id=1, source_target_pairs={{0,4},{4,8},{8,12},{12,16},{16,20},{20,24},{24,28},{28,0},{1,5},{5... | collective-permute-start | bytes 1179656 | tf_op jit(solution)/shard_map/ppermute | solution.py:24
  120.8 20.8 %copy-start.8 = (bf16[256,768]{1,0:T(8,128)(2,1)S(1)}, bf16[256,768]{1,0:T(8,128)(2,1)}, u32[]{:S(2)}) copy-start(bf16[256,768]{1,0:T(8,128)(2,1)} %get-tuple-element.261) | copy-start | bytes 1179652
  138.0 22.3 %collective-permute-start.4 = (bf16[256,768]{1,0:T(8,128)(2,1)}, bf16[256,768]{1,0:T(8,128)(2,1)}, u32[]{:S(2)}, u32[]{:S(2)}) collective-permute-start(bf16[256,768]{1,0:T(8,128)(2,1)} %collective-permute-done.2), channel_id=1, source_target_pairs={{0,4},{4,8},{8,12},{12,16},{16,20},{20,24},{24,28},{28,0},{1,5},{5... | collective-permute-start | bytes 1179656 | tf_op jit(solution)/shard_map/ppermute | solution.py:24
  142.5 5.5 copy-start.14
  150.0 31.7 %collective-permute-start.5 = (bf16[256,768]{1,0:T(8,128)(2,1)}, bf16[256,768]{1,0:T(8,128)(2,1)}, u32[]{:S(2)}, u32[]{:S(2)}) collective-permute-start(bf16[256,768]{1,0:T(8,128)(2,1)} %collective-permute-done.3), channel_id=1, source_target_pairs={{0,28},{4,0},{8,4},{12,8},{16,12},{20,16},{24,20},{28,24},{1,29},{... | collective-permute-start | bytes 1179656 | tf_op jit(solution)/shard_map/ppermute | solution.py:29
  160.3 25.9 %collective-permute-start.6 = (bf16[256,768]{1,0:T(8,128)(2,1)}, bf16[256,768]{1,0:T(8,128)(2,1)}, u32[]{:S(2)}, u32[]{:S(2)}) collective-permute-start(bf16[256,768]{1,0:T(8,128)(2,1)} %collective-permute-done.4), channel_id=1, source_target_pairs={{0,4},{4,8},{8,12},{12,16},{16,20},{20,24},{24,28},{28,0},{1,5},{5... | collective-permute-start | bytes 1179656 | tf_op jit(solution)/shard_map/ppermute | solution.py:24
  188.2 5.6 copy-start.13
  285.2 25.2 %copy-start.9 = (bf16[12,512,64]{1,2,0:T(8,128)(2,1)S(1)}, bf16[12,512,64]{1,2,0:T(8,128)(2,1)}, u32[]{:S(2)}) copy-start(bf16[12,512,64]{1,2,0:T(8,128)(2,1)} %get-tuple-element.103) | copy-start | bytes 2359300
  314.0 127.0 %copy-start.5 = (bf16[1,2,256,768]{3,2,1,0:T(8,128)(2,1)S(1)}, bf16[1,2,256,768]{3,2,1,0:T(8,128)(2,1)}, u32[]{:S(2)}) copy-start(bf16[1,2,256,768]{3,2,1,0:T(8,128)(2,1)} %param.31) | copy-start | bytes 2359300
  441.0 19.9 %copy-start.3 = (f32[512,768]{1,0:T(8,128)S(1)}, f32[512,768]{1,0:T(8,128)}, u32[]{:S(2)}) copy-start(f32[512,768]{1,0:T(8,128)} %copy-done.2) | copy-start | bytes 4718596
  441.0 19.9 %copy-start.36 = (bf16[768,3072]{1,0:T(8,128)(2,1)S(1)}, bf16[768,3072]{1,0:T(8,128)(2,1)}, u32[]{:S(2)}) copy-start(bf16[768,3072]{1,0:T(8,128)(2,1)} %all-gather.13.cloned.1.call-done) | copy-start | bytes 14155780
  460.8 3.4 copy-start.12
  464.3 3.1 copy-start.37
  629.2 151.6 %reduce-scatter.9.cloned.1.call-start = ((), (), s32[]{:S(2)}) async-start(), calls=%async_computation.13 | async-start | bytes 3538944 | tf_op jit(solution)/shard_map/reduce_scatter | solution.py:281
  633.2 4.6 copy-start.31
  633.2 251.7 %reduce-scatter.13.cloned.1.call-start = ((), (), s32[]{:S(2)}) async-start(), calls=%async_computation.15 | async-start | bytes 2433024 | tf_op jit(solution)/shard_map/reduce_scatter | solution.py:306
  637.8 389.0 %reduce-scatter.17.cloned.1.call-start = ((), (), s32[]{:S(2)}) async-start(), calls=%async_computation.17 | async-start | bytes 9732096 | tf_op jit(solution)/shard_map/reduce_scatter | solution.py:310
  647.9 519.9 %reduce-scatter.15.cloned.1.call-start = ((), (), s32[]{:S(2)}) async-start(), calls=%async_computation.16 | async-start | bytes 9732096 | tf_op jit(solution)/shard_map/reduce_scatter | solution.py:308
  656.4 47.7 %copy-start.18 = (f32[512,32]{0,1:T(8,128)S(1)}, f32[512,32]{0,1:T(8,128)}, u32[]{:S(2)}) copy-start(f32[512,32]{0,1:T(8,128)} %copy-done.17) | copy-start | bytes 196612
  656.4 47.7 %copy-start.20 = (f32[512,32]{0,1:T(8,128)S(1)}, f32[512,32]{0,1:T(8,128)}, u32[]{:S(2)}) copy-start(f32[512,32]{0,1:T(8,128)} %get-tuple-element.281) | copy-start | bytes 196612
  656.5 636.8 %reduce-scatter.11.cloned.1.call-start = ((), (), s32[]{:S(2)}) async-start(), calls=%async_computation.14 | async-start | bytes 7299072 | tf_op jit(solution)/shard_map/reduce_scatter | solution.py:305
  704.2 76.5 %copy-start.22 = (f32[512]{0:T(512)S(1)}, f32[512]{0:T(512)}, u32[]{:S(2)}) copy-start(f32[512]{0:T(512)} %copy-done.21) | copy-start | bytes 6148
  704.2 76.5 %copy-start.24 = (f32[512]{0:T(512)S(1)}, f32[512]{0:T(512)}, u32[]{:S(2)}) copy-start(f32[512]{0:T(512)} %copy-done.23) | copy-start | bytes 6148
  704.2 76.5 %copy-start.26 = (f32[768]{0:T(1024)S(1)}, f32[768]{0:T(1024)}, u32[]{:S(2)}) copy-start(f32[768]{0:T(1024)} %copy-done.25) | copy-start | bytes 9220
  706.5 74.3 %copy-start.19 = (bf16[256,12,64]{0,2,1:T(8,128)(2,1)S(1)}, bf16[256,12,64]{0,2,1:T(8,128)(2,1)}, u32[]{:S(2)}) copy-start(bf16[256,12,64]{0,2,1:T(8,128)(2,1)} %slice.124) | copy-start | bytes 1179652
  790.0 9.3 copy-start.7
  790.0 9.3 copy-start.15
  790.0 9.3 copy-start.16
  790.0 9.3 copy-start.38
  799.3 2.5 copy-start.28
  801.8 1.4 copy-start.1
  801.8 1.6 copy-start.6
  (10 other events, 11.8 us)
Sparse Core Ops, SparseCore 0:
  10.9 62.8 all-gather.6
  90.0 103.8 all-gather.8
  196.1 58.7 all-gather.16
  257.6 52.7 all-gather.10
  313.1 62.5 all-gather.12
  378.5 62.4 all-gather.14
  629.3 73.7 reduce-scatter.6
  706.7 73.9 reduce-scatter.8
  786.6 98.1 reduce-scatter.12
  892.2 134.4 reduce-scatter.16
  1033.2 134.4 reduce-scatter.14
  1174.8 118.4 reduce-scatter.10
